TPU v7x, 128 devices: a whole 4x4x4 slice. The times are simulated.
128 devices in a mesh: head: 8 (over x, y_hi), ctx: 16 (over y_lo, z, core).
Axes of the slice: x: 4, y: 4 (y_hi: 2, y_lo: 2; y = y_hi * 2 + y_lo), z: 4, core: 2. Of those that a mesh axis runs over, the one named last changes fastest.
Arguments:
- main_query: bfloat16 [2048, 73728], P('ctx', 'head'), may hold values from -400 to 400
- latent: bfloat16 [131072, 576], P('ctx'), may hold values from -20 to 20
- index_query: bfloat16 [2048, 8192], P('ctx', 'head'), may hold values from -400 to 400
- index_key: bfloat16 [131072, 128], P('ctx'), may hold values from -20 to 20
- index_weight: float32 [2048, 64], P('ctx', 'head'), may hold values from -0.1 to 0.1
- selected: int32 [2048, 32], P('ctx'), may hold values from 0 to 2047, as said below
- lengths: int32 [2048], P('ctx'), may hold values from 1985 to 131072
- cotangent: float32 [2048], P('ctx'), may hold values from 64 to 512
Outputs:
- index_query_grad: float32 [2048, 8192], P('ctx', 'head')
- index_weight_grad: float32 [2048, 64], P('ctx', 'head')
- index_key_grad: float32 [131072, 128], P('ctx')
Inputs may be any that keep to these rules, and one draw needn't show every extreme that they name: `selected`: each query names 32 distinct blocks in rising order, all holding at least one visible token; its last block holds its last visible token and all others are fully visible. The queries of one ctx index name exactly 64 distinct blocks in all, at most 8 of them among the tokens of any one ctx index, and exactly 8 among those of ctx index 0.
All inputs are finite; a program needn't handle non-finite values.
Results may differ from a plain program's by a relative error of at most 0.0026.
Values may be sent and summed in bfloat16 or wider, within the bound.
A program may use at most 128 MiB of HBM per device.

v0:
```python
import jax
import jax.numpy as jnp
from jax import lax
from jax.sharding import PartitionSpec as P

HEADS = 128
BLK = 64
POOL = 64
MOST = 8
logit_scale = 192.0 ** (-0.5)


def masked_softmax(values, visible):
    highest = jnp.max(jnp.where(visible, values, -jnp.inf), axis=-1, keepdims=True)
    weights = jnp.where(visible, jnp.exp(values - highest), 0.0)
    return weights / jnp.sum(weights, axis=-1, keepdims=True)


def row_product(left, right):
    return lax.dot_general(
        left, right, (((1,), (1,)), ((), ())), preferred_element_type=jnp.float32
    )


def shards(main_query, latent, index_query, index_key, index_weight, selected, lengths, cotangent):
    ctx_count = lax.axis_size("ctx")
    token_rows = latent.shape[0]
    latent_width = latent.shape[1]
    index_width = index_key.shape[1]
    blocks_each = token_rows // BLK
    block_total = ctx_count * blocks_each
    query_count = main_query.shape[0]
    main_heads = main_query.shape[1] // latent_width
    index_heads = index_weight.shape[1]
    union_rows = POOL * BLK
    block_numbers = jnp.arange(block_total, dtype=jnp.int32)
    present = jnp.any(selected.reshape(-1)[:, None] == block_numbers[None, :], axis=0)
    present_int = present.astype(jnp.int32)
    position = jnp.cumsum(present_int) - 1
    owner_rank = jnp.cumsum(present_int.reshape(ctx_count, blocks_each), axis=1) - 1
    union_index = jnp.arange(POOL, dtype=jnp.int32)
    block_ids = jnp.sum(
        jnp.where(
            present[None, :] & (position[None, :] == union_index[:, None]),
            block_numbers[None, :],
            0,
        ),
        axis=1,
    )
    source_slot = jnp.maximum(
        block_ids // blocks_each * MOST + owner_rank.reshape(-1)[block_ids], 0
    )
    local_ids = jnp.arange(blocks_each, dtype=jnp.int32)
    slot_numbers = jnp.arange(MOST, dtype=jnp.int32)
    requests = jnp.sum(
        jnp.where(
            present.reshape(ctx_count, blocks_each)[:, None, :]
            & (owner_rank[:, None, :] == slot_numbers[None, :, None]),
            local_ids[None, None, :],
            0,
        ),
        axis=2,
    )
    asked_blocks = lax.all_to_all(requests, "ctx", split_axis=0, concat_axis=0, tiled=True)
    latent_blocks = latent.reshape(blocks_each, BLK, latent_width)
    index_blocks = index_key.reshape(blocks_each, BLK, index_width)
    fetched_latent, fetched_index = (
        lax.all_to_all(latent_blocks[asked_blocks], "ctx", split_axis=0, concat_axis=0, tiled=True),
        lax.all_to_all(index_blocks[asked_blocks], "ctx", split_axis=0, concat_axis=0, tiled=True),
    )
    union_latent = fetched_latent.reshape(ctx_count * MOST, BLK, latent_width)[source_slot].reshape(
        union_rows, latent_width
    )
    union_index_key = fetched_index.reshape(ctx_count * MOST, BLK, index_width)[
        source_slot
    ].reshape(union_rows, index_width)
    slot_of_query = position[selected]
    member = jnp.any(slot_of_query[:, :, None] == union_index[None, None, :], axis=1)
    union_tokens = (block_ids[:, None] * BLK + jnp.arange(BLK, dtype=jnp.int32)[None, :]).reshape(
        -1
    )
    visible = jnp.repeat(member, BLK, axis=1) & (union_tokens[None, :] < lengths[:, None])
    step_rows = min(32, query_count)
    step_count = query_count // step_rows

    def blocked(array):
        return array.reshape((step_count, step_rows) + array.shape[1:])

    def forward_block(operands):
        query_block, indexer_block, weight_block, visible_block = operands
        score_matrix = row_product(
            query_block.reshape(step_rows * main_heads, latent_width), union_latent
        )
        score_matrix = score_matrix.reshape(step_rows, main_heads, union_rows) * logit_scale
        head_total = jnp.sum(masked_softmax(score_matrix, visible_block[:, None, :]), axis=1)
        raw_logits = row_product(
            indexer_block.reshape(step_rows * index_heads, index_width), union_index_key
        )
        raw_logits = raw_logits.reshape(step_rows, index_heads, union_rows)
        partial_scores = jnp.sum(weight_block[:, :, None] * jnp.maximum(raw_logits, 0.0), axis=1)
        return (head_total, partial_scores, raw_logits)

    head_total, partial_scores, stored_pre = lax.map(
        forward_block,
        (blocked(main_query), blocked(index_query), blocked(index_weight), blocked(visible)),
    )
    head_total = head_total.reshape(query_count, union_rows)
    partial_scores = partial_scores.reshape(query_count, union_rows)
    summed_probs, index_scores = lax.psum((head_total, partial_scores), "head")
    target = summed_probs / HEADS
    chosen = masked_softmax(index_scores, visible)
    grad_scores = cotangent[:, None] * (chosen - target)

    def backward_block(running, operands):
        indexer_block, weight_block, grad_block, raw_logits = operands
        weight_grad = jnp.sum(jnp.maximum(raw_logits, 0.0) * grad_block[:, None, :], axis=2)
        link_weights = jnp.where(
            raw_logits > 0, grad_block[:, None, :] * weight_block[:, :, None], 0.0
        ).astype(jnp.bfloat16)
        link_weights = link_weights.reshape(step_rows * index_heads, union_rows)
        query_gradient = jnp.dot(
            link_weights, union_index_key, preferred_element_type=jnp.float32
        ).reshape(step_rows, index_heads * index_width)
        running = running + lax.dot_general(
            link_weights,
            indexer_block.reshape(step_rows * index_heads, index_width),
            (((0,), (0,)), ((), ())),
            preferred_element_type=jnp.float32,
        )
        return (running, (query_gradient, weight_grad))

    union_grad, (query_gradient, weight_grad) = lax.scan(
        backward_block,
        jnp.zeros((union_rows, index_width), jnp.float32),
        (blocked(index_query), blocked(index_weight), blocked(grad_scores), stored_pre),
    )
    padded = (
        jnp.zeros((ctx_count * MOST, BLK, index_width), jnp.float32)
        .at[source_slot]
        .add(union_grad.reshape(POOL, BLK, index_width))
    )
    padded = padded.reshape(ctx_count, MOST, BLK, index_width)
    returned = lax.all_to_all(padded, "ctx", split_axis=0, concat_axis=0, tiled=True)
    owned_grad = (
        jnp.zeros((blocks_each, BLK, index_width), jnp.float32)
        .at[asked_blocks.reshape(-1)]
        .add(returned.reshape(ctx_count * MOST, BLK, index_width))
    )
    key_grad = lax.psum(owned_grad.reshape(token_rows, index_width), "head")
    return (
        query_gradient.reshape(query_count, index_heads * index_width),
        weight_grad.reshape(query_count, index_heads),
        key_grad,
    )


def solution(mesh):
    return jax.shard_map(
        shards,
        mesh=mesh,
        in_specs=(
            P("ctx", "head"),
            P("ctx", None),
            P("ctx", "head"),
            P("ctx", None),
            P("ctx", "head"),
            P("ctx", None),
            P("ctx"),
            P("ctx"),
        ),
        out_specs=(P("ctx", "head"), P("ctx", "head"), P("ctx", None)),
        check_vma=False,
    )
```

profile of v0, /device:TPU:4, one launch (start us, length us, event | category | flops | bytes accessed | tf_op | source)
XLA Modules:
  0.0 960.6 jit_solution(10510666388499681511)
XLA Ops:
  8.2 5.6 fusion.36
  14.7 12.3 %all_to_all.27 = s32[16,1,8]{2,1,0:T(1,128)S(1)} all-to-all(s32[16,1,8]{2,1,0:T(1,128)S(1)} %bitcast.164), channel_id=1, replica_groups=mesh['head'=8,'ctx'=16] {'ctx'}, dimensions={0} | all-to-all | bytes 1024 | tf_op jit(solution)/shard_map/all_to_all | solution.py:64
  29.9 3.7 all-to-all-start.2
  33.6 14.1 %copy.56 = bf16[8192,576]{1,0:T(8,128)(2,1)} copy(bf16[8192,576]{0,1:T(8,128)(2,1)} %param.13) | data formatting | bytes 18874368 | tf_op args[1]
  47.7 11.8 %gather_fusion.1 = bf16[128,64,576]{2,1,0:T(8,128)(2,1)} fusion(bf16[128,64,576]{2,1,0:T(8,128)(2,1)} %bitcast.148, s32[1024]{0:T(1024)S(1)} %pad_clamp_fusion.2), kind=kCustom, calls=%fused_computation.1 | custom fusion | bytes 18874880 | tf_op jit(solution)/shard_map/gather | solution.py:68
  59.5 2.9 all-to-all-done.2
  62.4 5.4 all-to-all-start.1
  68.6 23.0 %gather_fusion = s32[4096]{0:T(1024)S(1)} fusion(s32[2048]{0:T(1024)S(1)} %get-tuple-element.239, s32[4096]{0:T(1024)S(1)} %broadcast_clamp_fusion), kind=kCustom, calls=%fused_computation | custom fusion | bytes 49152 | tf_op jit(solution)/shard_map/gather | solution.py:77
  92.1 2.8 broadcast_in_dim.125.clone
  101.5 123.1 %all-to-all-done.1 = bf16[16,8,64,576]{3,2,1,0:T(8,128)(2,1)} async-done(((bf16[16,8,64,576]{3,2,1,0:T(8,128)(2,1)}), bf16[16,8,64,576]{3,2,1,0:T(8,128)(2,1)}, u32[]{:S(2)}, u32[]{:S(2)}) %all-to-all-start.1) | async-done | bytes 9437216 | tf_op jit(solution)/shard_map/all_to_all | solution.py:68
  224.6 7.5 gather_fusion.3
  232.1 7.7 copy.62
  239.8 162.8 %while.29 = (s32[]{:T(128)}, f32[4,32,4096]{2,1,0:T(8,128)}, f32[4,32,4096]{2,1,0:T(8,128)}, f32[4,32,8,4096]{3,2,1,0:T(8,128)}, pred[4,32,4096]{2,1,0:T(8,128)(...) while((s32[]{:T(128)}, f32[4,32,4096]{2,1,0:T(8,128)}, ...), condition=%wide.region_11.12_spmd, body=%wide.region_6.11_spmd.sunk | while | flops 2712417792 | bytes 67244160 | solution.py:103
  241.4 7.9 fusion.71
  250.3 12.7 %fusion.72 = f32[32,16,4096]{2,1,0:T(8,128)} fusion(f32[32,16,4096]{2,1,0:T(8,128)} %fusion.71, pred[32,4096]{1,0:T(8,128)(4,1)S(1)} %dynamic-slice_bitcast_fusion.7), kind=kOutput, calls=%fused_computation.8.clone.1 | output fusion | flops 10494974 | bytes 16908288 | tf_op jit(solution)/shard_map/while/body/eval_jaxpr/div | solution.py:16
  263.0 12.5 %divide_reduce_fusion.2 = f32[32,4096]{1,0:T(8,128)S(1)} fusion(f32[32,16,4096]{2,1,0:T(8,128)} %fusion.72, f32[32,16,4096]{2,1,0:T(8,128)} %fusion.71, pred[32,4096]{1,0:T(8,128)(4,1)S(1)} %dynamic-slice_bitcast_fusion.7), kind=kOutput, calls=%fused_computation.13.clone.1 | output fusion | flops 14553599 | bytes 17432576 | tf_op jit(solution)/shard_map/while/body/eval_jaxpr/sub | solution.py:15
  282.1 7.9 fusion.71
  290.9 12.7 %fusion.72 = f32[32,16,4096]{2,1,0:T(8,128)} fusion(f32[32,16,4096]{2,1,0:T(8,128)} %fusion.71, pred[32,4096]{1,0:T(8,128)(4,1)S(1)} %dynamic-slice_bitcast_fusion.7), kind=kOutput, calls=%fused_computation.8.clone.1 | output fusion | flops 10494974 | bytes 16908288 | tf_op jit(solution)/shard_map/while/body/eval_jaxpr/div | solution.py:16
  303.7 12.5 %divide_reduce_fusion.2 = f32[32,4096]{1,0:T(8,128)S(1)} fusion(f32[32,16,4096]{2,1,0:T(8,128)} %fusion.72, f32[32,16,4096]{2,1,0:T(8,128)} %fusion.71, pred[32,4096]{1,0:T(8,128)(4,1)S(1)} %dynamic-slice_bitcast_fusion.7), kind=kOutput, calls=%fused_computation.13.clone.1 | output fusion | flops 14553599 | bytes 17432576 | tf_op jit(solution)/shard_map/while/body/eval_jaxpr/sub | solution.py:15
  322.8 7.9 fusion.71
  331.7 12.7 %fusion.72 = f32[32,16,4096]{2,1,0:T(8,128)} fusion(f32[32,16,4096]{2,1,0:T(8,128)} %fusion.71, pred[32,4096]{1,0:T(8,128)(4,1)S(1)} %dynamic-slice_bitcast_fusion.7), kind=kOutput, calls=%fused_computation.8.clone.1 | output fusion | flops 10494974 | bytes 16908288 | tf_op jit(solution)/shard_map/while/body/eval_jaxpr/div | solution.py:16
  344.4 12.5 %divide_reduce_fusion.2 = f32[32,4096]{1,0:T(8,128)S(1)} fusion(f32[32,16,4096]{2,1,0:T(8,128)} %fusion.72, f32[32,16,4096]{2,1,0:T(8,128)} %fusion.71, pred[32,4096]{1,0:T(8,128)(4,1)S(1)} %dynamic-slice_bitcast_fusion.7), kind=kOutput, calls=%fused_computation.13.clone.1 | output fusion | flops 14553599 | bytes 17432576 | tf_op jit(solution)/shard_map/while/body/eval_jaxpr/sub | solution.py:15
  363.5 7.9 fusion.71
  372.4 12.7 %fusion.72 = f32[32,16,4096]{2,1,0:T(8,128)} fusion(f32[32,16,4096]{2,1,0:T(8,128)} %fusion.71, pred[32,4096]{1,0:T(8,128)(4,1)S(1)} %dynamic-slice_bitcast_fusion.7), kind=kOutput, calls=%fused_computation.8.clone.1 | output fusion | flops 10494974 | bytes 16908288 | tf_op jit(solution)/shard_map/while/body/eval_jaxpr/div | solution.py:16
  385.1 12.5 %divide_reduce_fusion.2 = f32[32,4096]{1,0:T(8,128)S(1)} fusion(f32[32,16,4096]{2,1,0:T(8,128)} %fusion.72, f32[32,16,4096]{2,1,0:T(8,128)} %fusion.71, pred[32,4096]{1,0:T(8,128)(4,1)S(1)} %dynamic-slice_bitcast_fusion.7), kind=kOutput, calls=%fused_computation.13.clone.1 | output fusion | flops 14553599 | bytes 17432576 | tf_op jit(solution)/shard_map/while/body/eval_jaxpr/sub | solution.py:15
  402.6 3.1 copy.63
  407.5 195.2 %all-reduce.6.cloned.1.call-done = (f32[128,4096]{0,1:T(8,128)}, f32[128,4096]{0,1:T(8,128)}) async-done(((f32[128,4096]{0,1:T(8,128)}, f32[128,4096]{0,1:T(8,128)}), (f32[128,4096]{0,1:T(8,128)}, f32[128,4096]{0,1:T(8,128)})) %all-reduce.6.cloned.1.call-update) | async-done | bytes 4194320 | tf_op jit(solution)/shard_map/psum | solution.py:109
  609.0 3.0 copy.65
  611.9 48.4 %while.30 = (s32[]{:T(128)}, f32[4096,128]{1,0:T(8,128)}, f32[4,32,1024]{2,1,0:T(8,128)}, f32[4,32,8]{2,1,0:T(8,128)S(1)}, f32[4,32,8,4096]{3,2,1,0:T(8,128)}, /...) while((s32[]{:T(128)}, f32[4096,128]{1,0:T(8,128)}, ...), condition=%wide.region_18.19_spmd.clone, body=%wide.region_16.18_spmd.clone.sunk | while | flops 548404992 | bytes 20453004 | solution.py:132
  613.0 2.7 fusion.77
  615.7 2.8 dynamic-slice_compare_fusion.2
  623.9 2.7 fusion.77
  626.6 2.8 dynamic-slice_compare_fusion.2
  629.5 4.1 convolution_add_fusion.2
  636.4 2.7 fusion.77
  639.1 2.8 dynamic-slice_compare_fusion.2
  642.0 4.1 convolution_add_fusion.2
  648.9 2.7 fusion.77
  651.6 2.8 dynamic-slice_compare_fusion.2
  654.5 4.1 convolution_add_fusion.2
  660.3 2.5 broadcast.212.clone
  662.9 9.0 scatter_fusion
  671.9 4.7 all-to-all-start.3
  677.9 54.9 %all-to-all-done.3 = f32[16,8,64,128]{3,2,1,0:T(8,128)} async-done(((f32[16,8,64,128]{3,2,1,0:T(8,128)}), f32[16,8,64,128]{3,2,1,0:T(8,128)}, u32[]{:S(2)}, u32[]{:S(2)}) %all-to-all-start.3) | async-done | bytes 4194336 | tf_op jit(solution)/shard_map/all_to_all | solution.py:143
  732.8 2.5 broadcast.212
  735.4 20.1 %scatter_fusion.1 = f32[128,64,128]{2,1,0:T(8,128)} fusion(f32[128,64,128]{2,1,0:T(8,128)} %broadcast.212, s32[128]{0:T(128)S(1)} %fusion.42, f32[128,64,128]{2,1,0:T(8,128)} %bitcast.36), kind=kCustom, calls=%fused_computation.7 | custom fusion | flops 1048576 | bytes 12583424 | tf_op jit(solution)/shard_map/scatter-add | solution.py:147
  756.1 193.0 %all-reduce.4.cloned.1.call-done = f32[8192,128]{1,0:T(8,128)} async-done(((f32[8192,128]{1,0:T(8,128)}), f32[8192,128]{1,0:T(8,128)}) %all-reduce.4.cloned.1.call-update) | async-done | bytes 4194320 | tf_op jit(solution)/shard_map/psum | solution.py:149
  949.1 4.6 copy.105
  (157 shorter events, 66.4 us)
Async XLA Ops:
  7.2 20.6 %copy-start = (bf16[8192,128]{1,0:T(8,128)(2,1)S(1)}, bf16[8192,128]{1,0:T(8,128)(2,1)}, u32[]{:S(2)}) copy-start(bf16[8192,128]{1,0:T(8,128)(2,1)} %param.15) | copy-start | bytes 6291460
  27.0 0.6 copy-start.7
  29.9 32.5 %all-to-all-start.2 = ((bf16[16,8,64,128]{3,2,1,0:T(8,128)(2,1)}), bf16[16,8,64,128]{3,2,1,0:T(8,128)(2,1)S(1)}, u32[]{:S(2)}, u32[]{:S(2)}) async-start(bf16[16,8,64,128]{3,2,1,0:T(8,128)(2,1)} %bitcast.154), calls=%async_computation.2 | async-start | bytes 4194304 | tf_op jit(solution)/shard_map/all_to_all | solution.py:69
  62.4 6.0 copy-start.9
  62.4 162.2 %all-to-all-start.1 = ((bf16[16,8,64,576]{3,2,1,0:T(8,128)(2,1)}), bf16[16,8,64,576]{3,2,1,0:T(8,128)(2,1)}, u32[]{:S(2)}, u32[]{:S(2)}) async-start(bf16[16,8,64,576]{3,2,1,0:T(8,128)(2,1)} %bitcast.147), calls=%async_computation.1 | async-start | bytes 20971520 | tf_op jit(solution)/shard_map/all_to_all | solution.py:68
  67.8 535.0 %all-reduce.6.cloned.1.call-start = ((), (), s32[]{:S(2)}) async-start(), calls=%async_computation.5 | async-start | bytes 8388608 | tf_op jit(solution)/shard_map/psum | solution.py:109
  68.6 28.8 %copy-start.11 = (s32[128]{0:T(128)S(1)}, s32[128]{0:T(128)}, u32[]{:S(2)}) copy-start(s32[128]{0:T(128)} %param.18) | copy-start | bytes 1540
  68.6 28.9 %copy-start.12 = (f32[128,8]{0,1:T(8,128)S(1)}, f32[128,8]{0,1:T(8,128)}, u32[]{:S(2)}) copy-start(f32[128,8]{0,1:T(8,128)} %param.16) | copy-start | bytes 12292
  98.4 133.7 %copy-start.13 = (s32[64]{0:T(128)}, s32[64]{0:T(128)S(1)}, u32[]{:S(2)}) copy-start(s32[64]{0:T(128)S(1)} %fusion.44) | copy-start | bytes 772
  232.1 7.7 copy-start.6
  402.6 3.1 copy-start.5
  407.5 199.3 %copy-start.15 = (f32[128]{0:T(128)S(1)}, f32[128]{0:T(128)}, u32[]{:S(2)}) copy-start(f32[128]{0:T(128)} %param.19) | copy-start | bytes 1540
  602.7 4.1 copy-start.2
  602.7 4.1 copy-start.4
  609.0 3.0 copy-start.10
  660.3 2.5 copy-start.3
  660.3 2.5 copy-start.14
  671.9 5.3 copy-start.8
  671.9 60.9 %all-to-all-start.3 = ((f32[16,8,64,128]{3,2,1,0:T(8,128)}), f32[16,8,64,128]{3,2,1,0:T(8,128)}, u32[]{:S(2)}, u32[]{:S(2)}) async-start(f32[16,8,64,128]{3,2,1,0:T(8,128)} %bitcast.151), calls=%async_computation.3 | async-start | bytes 8388608 | tf_op jit(solution)/shard_map/all_to_all | solution.py:143
  676.6 272.5 %all-reduce.4.cloned.1.call-start = ((), (), s32[]{:S(2)}) async-start(), calls=%async_computation.4 | async-start | bytes 8388608 | tf_op jit(solution)/shard_map/psum | solution.py:149
  949.1 4.6 copy-start.1
Sparse Core Ops, SparseCore 0:
  407.6 195.0 all-reduce.5
  755.6 193.4 all-reduce.3
where the time goes:
time: 963 us; the launch traced here: 961 us
  waiting for transfers between devices  569 us (59%)
  other arithmetic  168 us (17%)
  local copies, waits for them, and re-layouts  126 us (13%)
  matrix products  56.5 us (6%)
  between operations  14.3 us (1%)
  starting transfers between devices  14.1 us (1%)
  blocking collectives  12.3 us (1%)
    psum x1, waiting for transfers between devices, shards(): summed_probs, index_scores = lax.psum((head_total, partial_scores), 'head')  195 us
    psum x1, waiting for transfers between devices, shards(): key_grad = lax.psum(owned_grad.reshape(token_rows, index_width), 'head')  193 us
    all_to_all x1, waiting for transfers between devices, shards(): lax.all_to_all(latent_blocks[asked_blocks], 'ctx', split_axis=0, concat_a...  123 us
    all_to_all x1, waiting for transfers between devices, shards(): lax.all_to_all(padded, 'ctx', split_axis=0, concat_axis=0, tiled=True)  54.9 us
    div x4, other arithmetic, masked_softmax(): return weights / jnp.sum(weights, axis=-1, keepdims=True)  50.9 us
    sub x4, other arithmetic, masked_softmax(): weights = jnp.where(visible, jnp.exp(values - highest), 0.0)  50.1 us
    dot_general x8, matrix products, row_product(): lax.dot_general(left, right, (((1,), (1,)), ((), ())), preferred_element_...  38 us
    gather x3, local copies, waits for them, and re-layouts, shards(): slot_of_query = position[selected]  23.2 us
  transfers between devices with their start and end apart: 5, of which 5 were waited for; matrix products, arithmetic and copies ran while one was open for 6% of the time, Pallas kernels for 0%

commit v1 on v0

--- a/solution.py
+++ b/solution.py
@@ -146,7 +146,7 @@
         .at[asked_blocks.reshape(-1)]
         .add(returned.reshape(ctx_count * MOST, BLK, index_width))
     )
-    key_grad = lax.psum(owned_grad.reshape(token_rows, index_width), "head")
+    key_grad = jnp.sum(lax.all_gather(owned_grad.reshape(token_rows, index_width), "head"), axis=0)
     return (
         query_gradient.reshape(query_count, index_heads * index_width),
         weight_grad.reshape(query_count, index_heads),

time: 963 us -> 1120 us (1.16)
  waiting for transfers between devices: 569 us -> 719 us
  other arithmetic: 168 us -> 182 us
    all_gather x0 -> x1, waiting for transfers between devices: none -> 343 us  [shards(): lax.all_gather(owned_grad.reshape(token_rows, index_width), 'head')]
    psum x1 -> x0, waiting for transfers between devices: 193 us -> none  [shards(): key_grad = lax.psum(owned_grad.reshape(token_rows, index_width), 'head')]
    reduce_sum x0 -> x1, other arithmetic: none -> 14.1 us  [shards(): jnp.sum(lax.all_gather(owned_grad.reshape(token_rows, index_width), 'head...]
  transfers between devices with their start and end apart: 5 -> 5, of which waited for: 5 -> 5; matrix products, arithmetic and copies ran while one was open for 6% -> 5% of each run, Pallas kernels for 0% -> 0%
where the time goes in v1:
time: 1120 us
  waiting for transfers between devices  719 us (64%)
  other arithmetic  182 us (16%)
  local copies, waits for them, and re-layouts  121 us (11%)
  matrix products  56.5 us (5%)
  between operations  14.3 us (1%)
  starting transfers between devices  14.1 us (1%)
  blocking collectives  12.3 us (1%)
    all_gather x1, waiting for transfers between devices, shards(): lax.all_gather(owned_grad.reshape(token_rows, index_width), 'head')  343 us
    psum x1, waiting for transfers between devices, shards(): summed_probs, index_scores = lax.psum((head_total, partial_scores), 'head')  195 us
    all_to_all x1, waiting for transfers between devices, shards(): lax.all_to_all(latent_blocks[asked_blocks], 'ctx', split_axis=0, concat_a...  123 us
    all_to_all x1, waiting for transfers between devices, shards(): lax.all_to_all(padded, 'ctx', split_axis=0, concat_axis=0, tiled=True)  54.9 us
    div x4, other arithmetic, masked_softmax(): return weights / jnp.sum(weights, axis=-1, keepdims=True)  50.9 us
    sub x4, other arithmetic, masked_softmax(): weights = jnp.where(visible, jnp.exp(values - highest), 0.0)  50.1 us
    dot_general x8, matrix products, row_product(): lax.dot_general(left, right, (((1,), (1,)), ((), ())), preferred_element_...  38 us
    gather x3, local copies, waits for them, and re-layouts, shards(): slot_of_query = position[selected]  23.2 us
  transfers between devices with their start and end apart: 5, of which 5 were waited for; matrix products, arithmetic and copies ran while one was open for 5% of the time, Pallas kernels for 0%

profile of v1, /device:TPU:4, one launch (start us, length us, event | category | flops | bytes accessed | tf_op | source)
XLA Modules:
  0.0 1120.1 jit_solution(3043087361244022689)
XLA Ops:
  8.2 5.6 fusion.36
  14.7 12.3 %all_to_all.27 = s32[16,1,8]{2,1,0:T(1,128)S(1)} all-to-all(s32[16,1,8]{2,1,0:T(1,128)S(1)} %bitcast.164), channel_id=1, replica_groups=mesh['head'=8,'ctx'=16] {'ctx'}, dimensions={0} | all-to-all | bytes 1024 | tf_op jit(solution)/shard_map/all_to_all | solution.py:64
  29.9 3.7 all-to-all-start.2
  33.6 14.1 %copy.56 = bf16[8192,576]{1,0:T(8,128)(2,1)} copy(bf16[8192,576]{0,1:T(8,128)(2,1)} %param.13) | data formatting | bytes 18874368 | tf_op args[1]
  47.7 11.8 %gather_fusion.1 = bf16[128,64,576]{2,1,0:T(8,128)(2,1)} fusion(bf16[128,64,576]{2,1,0:T(8,128)(2,1)} %bitcast.148, s32[1024]{0:T(1024)S(1)} %pad_clamp_fusion.2), kind=kCustom, calls=%fused_computation.1 | custom fusion | bytes 18874880 | tf_op jit(solution)/shard_map/gather | solution.py:68
  59.5 2.9 all-to-all-done.2
  62.4 5.4 all-to-all-start.1
  68.6 23.0 %gather_fusion = s32[4096]{0:T(1024)S(1)} fusion(s32[2048]{0:T(1024)S(1)} %get-tuple-element.239, s32[4096]{0:T(1024)S(1)} %broadcast_clamp_fusion), kind=kCustom, calls=%fused_computation | custom fusion | bytes 49152 | tf_op jit(solution)/shard_map/gather | solution.py:77
  92.1 2.8 broadcast_in_dim.125.clone
  101.5 123.1 %all-to-all-done.1 = bf16[16,8,64,576]{3,2,1,0:T(8,128)(2,1)} async-done(((bf16[16,8,64,576]{3,2,1,0:T(8,128)(2,1)}), bf16[16,8,64,576]{3,2,1,0:T(8,128)(2,1)}, u32[]{:S(2)}, u32[]{:S(2)}) %all-to-all-start.1) | async-done | bytes 9437216 | tf_op jit(solution)/shard_map/all_to_all | solution.py:68
  224.6 7.5 gather_fusion.3
  232.1 7.7 copy.62
  239.8 162.8 %while.29 = (s32[]{:T(128)}, f32[4,32,4096]{2,1,0:T(8,128)}, f32[4,32,4096]{2,1,0:T(8,128)}, f32[4,32,8,4096]{3,2,1,0:T(8,128)}, pred[4,32,4096]{2,1,0:T(8,128)(...) while((s32[]{:T(128)}, f32[4,32,4096]{2,1,0:T(8,128)}, ...), condition=%wide.region_11.12_spmd, body=%wide.region_6.11_spmd.sunk | while | flops 2712417792 | bytes 67244160 | solution.py:103
  241.4 7.9 fusion.71
  250.3 12.7 %fusion.72 = f32[32,16,4096]{2,1,0:T(8,128)} fusion(f32[32,16,4096]{2,1,0:T(8,128)} %fusion.71, pred[32,4096]{1,0:T(8,128)(4,1)S(1)} %dynamic-slice_bitcast_fusion.7), kind=kOutput, calls=%fused_computation.8.clone.1 | output fusion | flops 10494974 | bytes 16908288 | tf_op jit(solution)/shard_map/while/body/eval_jaxpr/div | solution.py:16
  263.0 12.5 %divide_reduce_fusion.2 = f32[32,4096]{1,0:T(8,128)S(1)} fusion(f32[32,16,4096]{2,1,0:T(8,128)} %fusion.72, f32[32,16,4096]{2,1,0:T(8,128)} %fusion.71, pred[32,4096]{1,0:T(8,128)(4,1)S(1)} %dynamic-slice_bitcast_fusion.7), kind=kOutput, calls=%fused_computation.13.clone.1 | output fusion | flops 14553599 | bytes 17432576 | tf_op jit(solution)/shard_map/while/body/eval_jaxpr/sub | solution.py:15
  282.1 7.9 fusion.71
  290.9 12.7 %fusion.72 = f32[32,16,4096]{2,1,0:T(8,128)} fusion(f32[32,16,4096]{2,1,0:T(8,128)} %fusion.71, pred[32,4096]{1,0:T(8,128)(4,1)S(1)} %dynamic-slice_bitcast_fusion.7), kind=kOutput, calls=%fused_computation.8.clone.1 | output fusion | flops 10494974 | bytes 16908288 | tf_op jit(solution)/shard_map/while/body/eval_jaxpr/div | solution.py:16
  303.7 12.5 %divide_reduce_fusion.2 = f32[32,4096]{1,0:T(8,128)S(1)} fusion(f32[32,16,4096]{2,1,0:T(8,128)} %fusion.72, f32[32,16,4096]{2,1,0:T(8,128)} %fusion.71, pred[32,4096]{1,0:T(8,128)(4,1)S(1)} %dynamic-slice_bitcast_fusion.7), kind=kOutput, calls=%fused_computation.13.clone.1 | output fusion | flops 14553599 | bytes 17432576 | tf_op jit(solution)/shard_map/while/body/eval_jaxpr/sub | solution.py:15
  322.8 7.9 fusion.71
  331.7 12.7 %fusion.72 = f32[32,16,4096]{2,1,0:T(8,128)} fusion(f32[32,16,4096]{2,1,0:T(8,128)} %fusion.71, pred[32,4096]{1,0:T(8,128)(4,1)S(1)} %dynamic-slice_bitcast_fusion.7), kind=kOutput, calls=%fused_computation.8.clone.1 | output fusion | flops 10494974 | bytes 16908288 | tf_op jit(solution)/shard_map/while/body/eval_jaxpr/div | solution.py:16
  344.4 12.5 %divide_reduce_fusion.2 = f32[32,4096]{1,0:T(8,128)S(1)} fusion(f32[32,16,4096]{2,1,0:T(8,128)} %fusion.72, f32[32,16,4096]{2,1,0:T(8,128)} %fusion.71, pred[32,4096]{1,0:T(8,128)(4,1)S(1)} %dynamic-slice_bitcast_fusion.7), kind=kOutput, calls=%fused_computation.13.clone.1 | output fusion | flops 14553599 | bytes 17432576 | tf_op jit(solution)/shard_map/while/body/eval_jaxpr/sub | solution.py:15
  363.5 7.9 fusion.71
  372.4 12.7 %fusion.72 = f32[32,16,4096]{2,1,0:T(8,128)} fusion(f32[32,16,4096]{2,1,0:T(8,128)} %fusion.71, pred[32,4096]{1,0:T(8,128)(4,1)S(1)} %dynamic-slice_bitcast_fusion.7), kind=kOutput, calls=%fused_computation.8.clone.1 | output fusion | flops 10494974 | bytes 16908288 | tf_op jit(solution)/shard_map/while/body/eval_jaxpr/div | solution.py:16
  385.1 12.5 %divide_reduce_fusion.2 = f32[32,4096]{1,0:T(8,128)S(1)} fusion(f32[32,16,4096]{2,1,0:T(8,128)} %fusion.72, f32[32,16,4096]{2,1,0:T(8,128)} %fusion.71, pred[32,4096]{1,0:T(8,128)(4,1)S(1)} %dynamic-slice_bitcast_fusion.7), kind=kOutput, calls=%fused_computation.13.clone.1 | output fusion | flops 14553599 | bytes 17432576 | tf_op jit(solution)/shard_map/while/body/eval_jaxpr/sub | solution.py:15
  402.6 3.1 copy.63
  407.5 195.2 %all-reduce.3.cloned.1.call-done = (f32[128,4096]{0,1:T(8,128)}, f32[128,4096]{0,1:T(8,128)}) async-done(((f32[128,4096]{0,1:T(8,128)}, f32[128,4096]{0,1:T(8,128)}), (f32[128,4096]{0,1:T(8,128)}, f32[128,4096]{0,1:T(8,128)})) %all-reduce.3.cloned.1.call-update) | async-done | bytes 4194320 | tf_op jit(solution)/shard_map/psum | solution.py:109
  609.0 3.0 copy.65
  611.9 48.4 %while.30 = (s32[]{:T(128)}, f32[4096,128]{1,0:T(8,128)}, f32[4,32,1024]{2,1,0:T(8,128)}, f32[4,32,8]{2,1,0:T(8,128)S(1)}, f32[4,32,8,4096]{3,2,1,0:T(8,128)}, /...) while((s32[]{:T(128)}, f32[4096,128]{1,0:T(8,128)}, ...), condition=%wide.region_18.19_spmd.clone, body=%wide.region_16.18_spmd.clone.sunk | while | flops 548404992 | bytes 20453004 | solution.py:132
  613.0 2.7 fusion.77
  615.7 2.8 dynamic-slice_compare_fusion.2
  623.9 2.7 fusion.77
  626.6 2.8 dynamic-slice_compare_fusion.2
  629.5 4.1 convolution_add_fusion.2
  636.4 2.7 fusion.77
  639.1 2.8 dynamic-slice_compare_fusion.2
  642.0 4.1 convolution_add_fusion.2
  648.9 2.7 fusion.77
  651.6 2.8 dynamic-slice_compare_fusion.2
  654.5 4.1 convolution_add_fusion.2
  660.3 2.5 broadcast.212.clone
  662.9 9.0 scatter_fusion
  671.9 4.7 all-to-all-start.3
  677.9 54.9 %all-to-all-done.3 = f32[16,8,64,128]{3,2,1,0:T(8,128)} async-done(((f32[16,8,64,128]{3,2,1,0:T(8,128)}), f32[16,8,64,128]{3,2,1,0:T(8,128)}, u32[]{:S(2)}, u32[]{:S(2)}) %all-to-all-start.3) | async-done | bytes 4194336 | tf_op jit(solution)/shard_map/all_to_all | solution.py:143
  732.8 2.5 broadcast.212
  735.4 20.1 %scatter_fusion.1 = f32[128,64,128]{2,1,0:T(8,128)} fusion(f32[128,64,128]{2,1,0:T(8,128)} %broadcast.212, s32[128]{0:T(128)S(1)} %fusion.42, f32[128,64,128]{2,1,0:T(8,128)} %bitcast.36), kind=kCustom, calls=%fused_computation.7 | custom fusion | flops 1048576 | bytes 12583424 | tf_op jit(solution)/shard_map/scatter-add | solution.py:147
  756.1 343.0 %all-gather.2.cloned.1.call-done = f32[8,8192,128]{2,1,0:T(8,128)} async-done(((f32[1,8192,128]{2,1,0:T(8,128)}), f32[8,8192,128]{2,1,0:T(8,128)}) %all-gather.2.cloned.1.call-update) | async-done | bytes 33554448 | tf_op jit(solution)/shard_map/all_gather | solution.py:149
  1099.1 14.1 %reduce_sum.78 = f32[8192,128]{1,0:T(8,128)} reduce(f32[8,8192,128]{2,1,0:T(8,128)} %all-gather.2.cloned.1.call-done, f32[]{:T(128)} %constant.55.clone.1), dimensions={0}, to_apply=%region_21.22 | reduce | flops 7340032 | bytes 37748740 | tf_op jit(solution)/shard_map/reduce_sum | solution.py:149
  (157 shorter events, 66.4 us)
Async XLA Ops:
  7.2 20.6 %copy-start = (bf16[8192,128]{1,0:T(8,128)(2,1)S(1)}, bf16[8192,128]{1,0:T(8,128)(2,1)}, u32[]{:S(2)}) copy-start(bf16[8192,128]{1,0:T(8,128)(2,1)} %param.15) | copy-start | bytes 6291460
  27.0 0.6 copy-start.7
  29.9 32.5 %all-to-all-start.2 = ((bf16[16,8,64,128]{3,2,1,0:T(8,128)(2,1)}), bf16[16,8,64,128]{3,2,1,0:T(8,128)(2,1)S(1)}, u32[]{:S(2)}, u32[]{:S(2)}) async-start(bf16[16,8,64,128]{3,2,1,0:T(8,128)(2,1)} %bitcast.154), calls=%async_computation.2 | async-start | bytes 4194304 | tf_op jit(solution)/shard_map/all_to_all | solution.py:69
  62.4 6.0 copy-start.9
  62.4 162.2 %all-to-all-start.1 = ((bf16[16,8,64,576]{3,2,1,0:T(8,128)(2,1)}), bf16[16,8,64,576]{3,2,1,0:T(8,128)(2,1)}, u32[]{:S(2)}, u32[]{:S(2)}) async-start(bf16[16,8,64,576]{3,2,1,0:T(8,128)(2,1)} %bitcast.147), calls=%async_computation.1 | async-start | bytes 20971520 | tf_op jit(solution)/shard_map/all_to_all | solution.py:68
  67.8 535.0 %all-reduce.3.cloned.1.call-start = ((), (), s32[]{:S(2)}) async-start(), calls=%async_computation.5 | async-start | bytes 8388608 | tf_op jit(solution)/shard_map/psum | solution.py:109
  68.6 28.8 %copy-start.11 = (s32[128]{0:T(128)S(1)}, s32[128]{0:T(128)}, u32[]{:S(2)}) copy-start(s32[128]{0:T(128)} %param.18) | copy-start | bytes 1540
  68.6 28.9 %copy-start.12 = (f32[128,8]{0,1:T(8,128)S(1)}, f32[128,8]{0,1:T(8,128)}, u32[]{:S(2)}) copy-start(f32[128,8]{0,1:T(8,128)} %param.16) | copy-start | bytes 12292
  98.4 133.7 %copy-start.13 = (s32[64]{0:T(128)}, s32[64]{0:T(128)S(1)}, u32[]{:S(2)}) copy-start(s32[64]{0:T(128)S(1)} %fusion.44) | copy-start | bytes 772
  232.1 7.7 copy-start.6
  402.6 3.1 copy-start.5
  407.5 199.3 %copy-start.15 = (f32[128]{0:T(128)S(1)}, f32[128]{0:T(128)}, u32[]{:S(2)}) copy-start(f32[128]{0:T(128)} %param.19) | copy-start | bytes 1540
  602.7 4.1 copy-start.2
  602.7 4.1 copy-start.4
  609.0 3.0 copy-start.10
  660.3 2.5 copy-start.3
  660.3 2.5 copy-start.14
  671.9 5.3 copy-start.8
  671.9 60.9 %all-to-all-start.3 = ((f32[16,8,64,128]{3,2,1,0:T(8,128)}), f32[16,8,64,128]{3,2,1,0:T(8,128)}, u32[]{:S(2)}, u32[]{:S(2)}) async-start(f32[16,8,64,128]{3,2,1,0:T(8,128)} %bitcast.151), calls=%async_computation.3 | async-start | bytes 8388608 | tf_op jit(solution)/shard_map/all_to_all | solution.py:143
  676.6 422.6 %all-gather.2.cloned.1.call-start = ((), (), s32[]{:S(2)}) async-start(), calls=%async_computation.4 | async-start | bytes 37748736 | tf_op jit(solution)/shard_map/all_gather | solution.py:149
  1099.1 14.1 %copy-start.1 = (bf16[8192,128]{1,0:T(8,128)(2,1)S(1)}, bf16[8192,128]{1,0:T(8,128)(2,1)}, u32[]{:S(2)}) copy-start(bf16[8192,128]{1,0:T(8,128)(2,1)} %param.15) | copy-start | bytes 6291460
Sparse Core Ops, SparseCore 0:
  407.6 195.0 all-reduce.2
  755.6 343.5 all-gather.1
